TPU v7x, 32 devices: a whole 2x2x4 slice. The times are simulated.
32 devices in a mesh: dp: 16 (over z, x, core), mp: 2 (over y).
Axes of the slice: x: 2, y: 2, z: 4, core: 2. Of those that a mesh axis runs over, the one named last changes fastest.
Arguments:
- tokens: bfloat16 [64, 256, 1152], P('dp'), may hold values from -6 to 6
- conditioning: bfloat16 [64, 1152], P('dp'), may hold values from -6 to 6
- bucket_ids: int32 [64], P('dp'), may hold values from 0 to 2, as said below
- keep_order: int32 [64, 128], P('dp'), may hold values from 0 to 255, as said below
- group_counts: int32 [16], P('dp'), may hold values from 1 to 4, as said below
- cotangent: bfloat16 [64, 256, 1152], P('dp'), may hold values from -6 to 6
- modulation_weight: bfloat16 [1152, 6912], P('dp'), may hold values from -0.1875 to 0.1875
- modulation_bias: bfloat16 [6912], replicated, may hold values from -3 to 3
- input_weight: bfloat16 [3, 1152, 1152], P(None, 'dp', 'mp'), may hold values from -0.1875 to 0.1875
- query_value_bias: bfloat16 [2, 1152], P(None, 'mp'), may hold values from -3 to 3
- output_weight: bfloat16 [1152, 1152], P('mp', 'dp'), may hold values from -0.75 to 0.75
- output_bias: bfloat16 [1152], replicated, may hold values from -2 to 2
- expand_weight: bfloat16 [1152, 4608], P('dp', 'mp'), may hold values from -0.1875 to 0.1875
- expand_bias: bfloat16 [4608], P('mp'), may hold values from -3 to 3
- shrink_weight: bfloat16 [4608, 1152], P('mp', 'dp'), may hold values from -0.09375 to 0.09375
- shrink_bias: bfloat16 [1152], replicated, may hold values from -2 to 2
Outputs:
- block_out: bfloat16 [64, 256, 1152], P('dp')
- tokens_grad: bfloat16 [64, 256, 1152], P('dp')
- modulation_weight_grad: float32 [1152, 6912], P('dp')
- modulation_bias_grad: float32 [6912], replicated
- input_weight_grad: float32 [3, 1152, 1152], P(None, 'dp', 'mp')
- query_value_bias_grad: float32 [2, 1152], P(None, 'mp')
- output_weight_grad: float32 [1152, 1152], P('mp', 'dp')
- output_bias_grad: float32 [1152], replicated
- expand_weight_grad: float32 [1152, 4608], P('dp', 'mp')
- expand_bias_grad: float32 [4608], P('mp')
- shrink_weight_grad: float32 [4608, 1152], P('mp', 'dp')
- shrink_bias_grad: float32 [1152], replicated
Inputs may be any that keep to these rules, and one draw needn't show every extreme that they name: `bucket_ids`: buckets 0, 1 and 2 stand for grids of 16 x 16, 12 x 20 and 20 x 12 patches. `keep_order`: row i holds 128 distinct slot numbers; its first valid-length entries (half of image i's length) are real token slots of that image chosen at random, the remaining entries are other slots of that image. Group g holds live images in its first group_counts[g] of 4 image slots; in every draw some group is full.
All inputs are finite; a program needn't handle non-finite values.
Results may differ from a plain program's by a relative error of at most 0.015.
The roundings to bfloat16 on the way count: a program that leaves them out, or rounds other values in their place, can miss the bound.
Values may be sent and summed in bfloat16 or wider, within the bound.
A program may use at most 144 MiB of HBM per device.

v0:
```python
import jax
import jax.numpy as jnp
from jax import lax
from jax.sharding import PartitionSpec as P

HEAD_DIM = 72
MICRO = 2
EPSILON = 1e-06


def normalize(rows):
    center = rows - jnp.mean(rows, axis=-1, keepdims=True)
    spread = jnp.mean(center * center, axis=-1, keepdims=True)
    return center * lax.rsqrt(spread + EPSILON)


def modulated(rows, shift, scale):
    return normalize(rows) * (1.0 + scale) + shift


def gelu_tanh(values):
    return jax.nn.gelu(values, approximate=True)


def model_total_sum(partial_value):
    share = lax.psum_scatter(partial_value, "mp", scatter_dimension=2, tiled=True)
    return lax.all_gather(share, "mp", axis=2, tiled=True)


def gather_weights(modulation_weight, input_weight, output_weight, expand_weight, shrink_weight):
    return (
        lax.all_gather(modulation_weight, "dp", axis=0, tiled=True),
        lax.all_gather(input_weight, "dp", axis=1, tiled=True),
        lax.all_gather(output_weight, "dp", axis=1, tiled=True),
        lax.all_gather(expand_weight, "dp", axis=0, tiled=True),
        lax.all_gather(shrink_weight, "dp", axis=1, tiled=True),
    )


def scatter_every(terms):
    return (
        lax.psum_scatter(terms[0], "dp", scatter_dimension=0, tiled=True),
        lax.psum_scatter(terms[1], "dp", scatter_dimension=1, tiled=True),
        lax.psum_scatter(terms[2], "dp", scatter_dimension=1, tiled=True),
        lax.psum_scatter(terms[3], "dp", scatter_dimension=0, tiled=True),
        lax.psum_scatter(terms[4], "dp", scatter_dimension=1, tiled=True),
    )


def attention_scores(query, key_rows, keymask, scale_factor):
    scores = (
        jnp.einsum("bqhd,bkhd->bhqk", query, key_rows, preferred_element_type=jnp.float32)
        * scale_factor
    )
    return jnp.where(keymask[:, None, None, :], scores, -1e30)


def run_micro(tokens_mb, cond_mb, order_mb, valid_mb, grad_mb, full, biases):
    mod_w, incoming_weight, outgoing_weight, expert_weight_rows, narrowing_weight = full
    mod_bias, qv_bias, outgoing_bias, expert_bias_rows, narrowing_bias = biases
    batch, keep = order_mb.shape
    width = tokens_mb.shape[2]
    inner = incoming_weight.shape[2]
    heads_here = inner // HEAD_DIM
    scale_factor = HEAD_DIM ** (-0.5)
    single_float32 = jnp.float32
    bf16 = jnp.bfloat16
    batch_rows = jnp.arange(batch)[:, None]
    keymask = jnp.arange(keep)[None, :] < valid_mb[:, None]
    rowmask = keymask[:, :, None]
    hidden_in = jnp.take_along_axis(tokens_mb, order_mb[:, :, None], axis=1).astype(single_float32)
    silu_cond = jax.nn.silu(cond_mb.astype(single_float32)).astype(bf16)
    modulation = jnp.dot(silu_cond, mod_w, preferred_element_type=single_float32) + mod_bias
    pieces = modulation.reshape(batch, 6, 1, width)
    shift_one, scale_one, gate_one = (pieces[:, 0], pieces[:, 1], pieces[:, 2])
    shift_two, scale_two, gate_two = (pieces[:, 3], pieces[:, 4], pieces[:, 5])
    first, pull_first = jax.vjp(modulated, hidden_in, shift_one, scale_one)
    first_reduced = first.astype(bf16)
    projected_rows = jnp.einsum(
        "mzu,lug->lmzg", first_reduced, incoming_weight, preferred_element_type=single_float32
    )
    query = (projected_rows[0] + qv_bias[0]).astype(bf16).reshape(batch, keep, heads_here, HEAD_DIM)
    key_rows = projected_rows[1].astype(bf16).reshape(batch, keep, heads_here, HEAD_DIM)
    value = (projected_rows[2] + qv_bias[1]).astype(bf16).reshape(batch, keep, heads_here, HEAD_DIM)
    scores = attention_scores(query, key_rows, keymask, scale_factor)
    top = jnp.max(scores, axis=-1, keepdims=True)
    expo = jnp.exp(scores - top)
    total = jnp.sum(expo, axis=-1, keepdims=True)
    probs = expo / total
    log_total = top + jnp.log(total)
    attention_result = (
        jnp.einsum(
            "bhqk,bkhd->bqhd", probs.astype(bf16), value, preferred_element_type=single_float32
        )
        .astype(bf16)
        .reshape(batch, keep, inner)
    )
    attn_out = (
        model_total_sum(
            jnp.einsum(
                "hfc,cj->hfj",
                attention_result,
                outgoing_weight,
                preferred_element_type=single_float32,
            )
        )
        + outgoing_bias
    )
    middle = hidden_in + gate_one * attn_out
    second, pull_second = jax.vjp(modulated, middle, shift_two, scale_two)
    second_reduced = second.astype(bf16)
    preactivation_rows = (
        jnp.einsum(
            "get,tm->gem", second_reduced, expert_weight_rows, preferred_element_type=single_float32
        )
        + expert_bias_rows
    )
    activated, pull_act = jax.vjp(gelu_tanh, preactivation_rows)
    activation_reduced = activated.astype(bf16)
    mlp_out = (
        model_total_sum(
            jnp.einsum(
                "xwl,lc->xwc",
                activation_reduced,
                narrowing_weight,
                preferred_element_type=single_float32,
            )
        )
        + narrowing_bias
    )
    routed_out = jnp.where(rowmask, middle + gate_two * mlp_out, hidden_in)
    block_mb = tokens_mb.at[batch_rows, order_mb].set(routed_out.astype(bf16))
    grad_rows = jnp.take_along_axis(grad_mb, order_mb[:, :, None], axis=1).astype(single_float32)
    grad_final = jnp.where(rowmask, grad_rows, 0.0)
    grad_skip = grad_rows - grad_final
    grad_gate_two = jnp.sum(mlp_out * grad_final, axis=1, keepdims=True)
    grad_mlp = gate_two * grad_final
    perceptron_gradient_reduced = grad_mlp.astype(bf16)
    narrowing_term = jnp.einsum(
        "ehm,eht->mt",
        activation_reduced,
        perceptron_gradient_reduced,
        preferred_element_type=single_float32,
    )
    (grad_pre,) = pull_act(
        jnp.einsum(
            "awm,hm->awh",
            perceptron_gradient_reduced,
            narrowing_weight,
            preferred_element_type=single_float32,
        )
    )
    preactivation_gradient_reduced = grad_pre.astype(bf16)
    widening_term = jnp.einsum(
        "cnq,cne->qe",
        second_reduced,
        preactivation_gradient_reduced,
        preferred_element_type=single_float32,
    )
    grad_second = model_total_sum(
        jnp.einsum(
            "pem,sm->pes",
            preactivation_gradient_reduced,
            expert_weight_rows,
            preferred_element_type=single_float32,
        )
    )
    grad_middle, grad_shift_two, grad_scale_two = pull_second(grad_second)
    grad_middle = grad_middle + grad_final
    grad_gate_one = jnp.sum(attn_out * grad_middle, axis=1, keepdims=True)
    grad_attn = gate_one * grad_middle
    attention_gradient_reduced = grad_attn.astype(bf16)
    output_summand = jnp.einsum(
        "tyo,tyq->oq",
        attention_result,
        attention_gradient_reduced,
        preferred_element_type=single_float32,
    )
    grad_attended = (
        jnp.einsum(
            "znx,ox->zno",
            attention_gradient_reduced,
            outgoing_weight,
            preferred_element_type=single_float32,
        )
        .astype(bf16)
        .reshape(batch, keep, heads_here, HEAD_DIM)
    )
    again = attention_scores(query, key_rows, keymask, scale_factor)
    probs_again = jnp.exp(again - log_total)
    grad_probs = jnp.einsum(
        "bqhd,bkhd->bhqk", grad_attended, value, preferred_element_type=single_float32
    )
    grad_value = jnp.einsum(
        "bhqk,bqhd->bkhd",
        probs_again.astype(bf16),
        grad_attended,
        preferred_element_type=single_float32,
    )
    inner_sum = jnp.sum(probs_again * grad_probs, axis=-1, keepdims=True)
    grad_scores = (probs_again * (grad_probs - inner_sum)).astype(bf16)
    grad_query = (
        jnp.einsum("bhqk,bkhd->bqhd", grad_scores, key_rows, preferred_element_type=single_float32)
        * scale_factor
    )
    grad_key = (
        jnp.einsum("bhqk,bqhd->bkhd", grad_scores, query, preferred_element_type=single_float32)
        * scale_factor
    )
    grad_proj = jnp.stack([grad_query, grad_key, grad_value]).reshape(3, batch, keep, inner)
    query_value_term = jnp.sum(grad_proj[::2], axis=(1, 2))
    projection_gradient_reduced = grad_proj.astype(bf16)
    input_summand = jnp.einsum(
        "iyj,fiyu->fju",
        first_reduced,
        projection_gradient_reduced,
        preferred_element_type=single_float32,
    )
    grad_first = model_total_sum(
        jnp.einsum(
            "pniu,psu->nis",
            projection_gradient_reduced,
            incoming_weight,
            preferred_element_type=single_float32,
        )
    )
    grad_hidden, grad_shift_one, grad_scale_one = pull_first(grad_first)
    grad_total = grad_hidden + grad_middle + grad_skip
    tokens_mb_grad = grad_mb.at[batch_rows, order_mb].set(grad_total.astype(bf16))
    grad_mod = jnp.concatenate(
        [
            grad_shift_one,
            grad_scale_one,
            grad_gate_one,
            grad_shift_two,
            grad_scale_two,
            grad_gate_two,
        ],
        axis=1,
    ).reshape(batch, 6 * width)
    terms = (input_summand, output_summand, widening_term, narrowing_term)
    bias_terms = (
        jnp.sum(grad_mod, axis=0),
        query_value_term,
        jnp.sum(grad_attn, axis=(0, 1)),
        jnp.sum(grad_pre, axis=(0, 1)),
        jnp.sum(grad_mlp, axis=(0, 1)),
    )
    return (block_mb, tokens_mb_grad, terms, bias_terms, silu_cond, grad_mod.astype(bf16))


def body(
    tokens,
    conditioning,
    bucket_ids,
    keep_order,
    group_counts,
    cotangent,
    modulation_weight,
    modulation_bias,
    input_weight,
    query_value_bias,
    output_weight,
    output_bias,
    expand_weight,
    expand_bias,
    shrink_weight,
    shrink_bias,
):
    local = tokens.shape[0]
    per_micro = local // MICRO
    slots = tokens.shape[1]
    lengths = jnp.where(bucket_ids == 0, slots, slots - slots // 16) // 2
    valid = jnp.where(jnp.arange(local) < group_counts[0], lengths, 0).astype(jnp.int32)
    biases = (
        modulation_bias.astype(jnp.float32),
        query_value_bias.astype(jnp.float32),
        output_bias.astype(jnp.float32),
        expand_bias.astype(jnp.float32),
        shrink_bias.astype(jnp.float32),
    )
    block_parts = []
    grad_parts = []
    weight_sums = None
    bias_sums = None
    for micro in range(MICRO):
        full = gather_weights(
            modulation_weight, input_weight, output_weight, expand_weight, shrink_weight
        )
        begin = micro * per_micro
        finish = begin + per_micro
        block_mb, grad_mb, terms, bias_terms, silu_cond, grad_mod_low = run_micro(
            tokens[begin:finish],
            conditioning[begin:finish],
            keep_order[begin:finish],
            valid[begin:finish],
            cotangent[begin:finish],
            full,
            biases,
        )
        block_parts.append(block_mb)
        grad_parts.append(grad_mb)
        mod_term = jnp.einsum(
            "bd,be->de", silu_cond, grad_mod_low, preferred_element_type=jnp.float32
        )
        terms = (mod_term,) + tuple(terms)
        terms = scatter_every(terms)
        if weight_sums is None:
            weight_sums = tuple(terms)
            bias_sums = bias_terms
        else:
            weight_sums = tuple((left + right for left, right in zip(weight_sums, terms)))
            bias_sums = tuple((left + right for left, right in zip(bias_sums, bias_terms)))
    bias_sums = lax.psum(
        (bias_sums[0], bias_sums[1], bias_sums[2], bias_sums[3], bias_sums[4]), "dp"
    )
    return (
        jnp.concatenate(block_parts, axis=0),
        jnp.concatenate(grad_parts, axis=0),
        weight_sums[0],
        bias_sums[0],
        weight_sums[1],
        bias_sums[1],
        weight_sums[2],
        bias_sums[2],
        weight_sums[3],
        bias_sums[3],
        weight_sums[4],
        bias_sums[4],
    )


def solution(mesh):
    in_specs = (
        P("dp", None, None),
        P("dp", None),
        P("dp"),
        P("dp", None),
        P("dp"),
        P("dp", None, None),
        P("dp", None),
        P(),
        P(None, "dp", "mp"),
        P(None, "mp"),
        P("mp", "dp"),
        P(),
        P("dp", "mp"),
        P("mp"),
        P("mp", "dp"),
        P(),
    )
    out_specs = (
        P("dp", None, None),
        P("dp", None, None),
        P("dp", None),
        P(),
        P(None, "dp", "mp"),
        P(None, "mp"),
        P("mp", "dp"),
        P(),
        P("dp", "mp"),
        P("mp"),
        P("mp", "dp"),
        P(),
    )
    return jax.shard_map(body, mesh=mesh, in_specs=in_specs, out_specs=out_specs, check_vma=False)
```

profile of v0, /device:TPU:0, one launch (start us, length us, event | category | flops | bytes accessed | tf_op | source)
XLA Modules:
  0.0 1631.6 jit_solution(14965664791636846735)
XLA Ops:
  18.7 115.8 %all-gather.14.cloned.1.call-done = bf16[1152,6912]{1,0:T(8,128)(2,1)} async-done(((bf16[72,6912]{1,0:T(8,128)(2,1)}), bf16[1152,6912]{1,0:T(8,128)(2,1)}) %all-gather.14.cloned.1.call-update) | async-done | bytes 15925264 | tf_op jit(solution)/shard_map/all_gather | solution.py:32
  134.5 7.7 convolution_add_fusion.2
  142.3 44.3 %all-gather.16.cloned.1.call-done = bf16[3,1152,576]{2,1,0:T(8,128)(2,1)} async-done(((bf16[3,72,576]{2,1,0:T(8,128)(2,1)}), bf16[3,1152,576]{2,1,0:T(8,128)(2,1)}) %all-gather.16.cloned.1.call-update) | async-done | bytes 3981328 | tf_op jit(solution)/shard_map/all_gather | solution.py:33
  193.7 33.0 %all-gather.18.cloned.1.call-done = bf16[576,1152]{0,1:T(8,128)(2,1)} async-done(((bf16[576,72]{0,1:T(8,128)(2,1)}), bf16[576,1152]{0,1:T(8,128)(2,1)}) %all-gather.18.cloned.1.call-update) | async-done | bytes 1327120 | tf_op jit(solution)/shard_map/all_gather | solution.py:34
  229.8 20.7 %reduce-scatter.15.cloned.1.call-done = f32[2,128,576]{1,2,0:T(8,128)} async-done(((f32[2,128,1152]{1,2,0:T(8,128)}), f32[2,128,576]{1,2,0:T(8,128)}) %reduce-scatter.15.cloned.1.call-update) | async-done | bytes 589840 | tf_op jit(solution)/shard_map/reduce_scatter | solution.py:26
  267.5 7.3 all-gather.20.cloned.1.call-done
  278.5 54.9 %all-gather.22.cloned.1.call-done = bf16[1152,2304]{1,0:T(8,128)(2,1)} async-done(((bf16[72,2304]{1,0:T(8,128)(2,1)}), bf16[1152,2304]{1,0:T(8,128)(2,1)}) %all-gather.22.cloned.1.call-update) | async-done | bytes 5308432 | tf_op jit(solution)/shard_map/all_gather | solution.py:35
  339.2 51.5 %all-gather.24.cloned.1.call-done = bf16[2304,1152]{0,1:T(8,128)(2,1)} async-done(((bf16[2304,72]{0,1:T(8,128)(2,1)}), bf16[2304,1152]{0,1:T(8,128)(2,1)}) %all-gather.24.cloned.1.call-update) | async-done | bytes 5308432 | tf_op jit(solution)/shard_map/all_gather | solution.py:36
  390.8 7.1 fusion.194
  401.8 8.7 convolution_add_fusion.1
  431.2 15.4 reduce-scatter.19.cloned.1.call-done
  447.8 23.2 %all-gather.32.cloned.1.call-done = f32[2,128,1152]{1,2,0:T(8,128)} async-done(((f32[2,128,576]{1,2,0:T(8,128)}), f32[2,128,1152]{1,2,0:T(8,128)}) %all-gather.32.cloned.1.call-update) | async-done | bytes 1179664 | tf_op jit(solution)/shard_map/all_gather | solution.py:27
  475.0 20.4 %all-gather.28.cloned.1.call-done = f32[2,128,1152]{1,2,0:T(8,128)} async-done(((f32[2,128,576]{1,2,0:T(8,128)}), f32[2,128,1152]{1,2,0:T(8,128)}) %all-gather.28.cloned.1.call-update) | async-done | bytes 1179664 | tf_op jit(solution)/shard_map/all_gather | solution.py:27
  506.4 7.2 fusion.195
  517.3 21.9 %reduce-scatter.27.cloned.1.call-done = f32[2,128,576]{1,2,0:T(8,128)} async-done(((f32[2,128,1152]{1,2,0:T(8,128)}), f32[2,128,576]{1,2,0:T(8,128)}) %reduce-scatter.27.cloned.1.call-update) | async-done | bytes 589840 | tf_op jit(solution)/shard_map/reduce_scatter | solution.py:26
  587.5 23.9 %reduce-scatter.25.cloned.1.call-done = f32[2,128,576]{1,2,0:T(8,128)} async-done(((f32[2,128,1152]{1,2,0:T(8,128)}), f32[2,128,576]{1,2,0:T(8,128)}) %reduce-scatter.25.cloned.1.call-update) | async-done | bytes 589840 | tf_op jit(solution)/shard_map/reduce_scatter | solution.py:26
  611.4 24.4 %reduce-scatter.21.cloned.1.call-done = f32[2,128,576]{1,2,0:T(8,128)} async-done(((f32[2,128,1152]{1,2,0:T(8,128)}), f32[2,128,576]{1,2,0:T(8,128)}) %reduce-scatter.21.cloned.1.call-update) | async-done | bytes 589840 | tf_op jit(solution)/shard_map/reduce_scatter | solution.py:26
  635.9 23.9 %reduce-scatter.29.cloned.1.call-done = f32[2,128,576]{1,2,0:T(8,128)} async-done(((f32[2,128,1152]{1,2,0:T(8,128)}), f32[2,128,576]{1,2,0:T(8,128)}) %reduce-scatter.29.cloned.1.call-update) | async-done | bytes 589840 | tf_op jit(solution)/shard_map/reduce_scatter | solution.py:26
  667.9 13.8 copy.156
  717.3 12.5 fusion.178
  732.5 24.4 %all-gather.38.cloned.1.call-done = f32[2,128,1152]{1,2,0:T(8,128)} async-done(((f32[2,128,576]{1,2,0:T(8,128)}), f32[2,128,1152]{1,2,0:T(8,128)}) %all-gather.38.cloned.1.call-update) | async-done | bytes 1179664 | tf_op jit(solution)/shard_map/all_gather | solution.py:27
  763.7 25.0 %convolution_add_fusion = f32[1152,6912]{1,0:T(8,128)} fusion(f32[1152,6912]{1,0:T(8,128)} %fusion.178, bf16[2,6912]{1,0:T(2,128)(2,1)S(1)} %bitcast.353, bf16[4,1152]{1,0:T(4,128)(2,1)S(1)} %copy-done.78), kind=kOutput, calls=%fused_computation.8 | convolution fusion | flops 39826944 | bytes 63733248 | tf_op jit(solution)/shard_map/bd,be->de/dot_general | solution.py:303
  798.2 17.7 %scatter_fusion.2 = bf16[2,256,1152]{2,1,0:T(8,128)(2,1)S(1)} fusion(bf16[2,256,1152]{2,1,0:T(8,128)(2,1)S(1)} %copy-done.7, s32[256]{0:T(256)S(1)} %copy-done.10, bf16[256,1152]{1,0:T(8,128)(2,1)S(1)} %bitcast.322), kind=kCustom, calls=%fused_computation.6 | custom fusion | bytes 1771520 | tf_op jit(solution)/shard_map/scatter | solution.py:229
  816.0 26.8 %scatter_fusion = bf16[2,256,1152]{2,1,0:T(8,128)(2,1)S(1)} fusion(bf16[2,256,1152]{2,1,0:T(8,128)(2,1)S(1)} %copy-done.3, s32[256]{0:T(256)S(1)} %copy-done.10, bf16[256,1152]{1,0:T(8,128)(2,1)} %bitcast.321), kind=kCustom, calls=%fused_computation.4 | custom fusion | bytes 1771520 | tf_op jit(solution)/shard_map/scatter | solution.py:132
  852.4 26.6 %scatter_fusion.3 = bf16[2,256,1152]{2,1,0:T(8,128)(2,1)S(1)} fusion(bf16[2,256,1152]{2,1,0:T(8,128)(2,1)S(1)} %copy-done.5, s32[256]{0:T(256)S(1)} %copy-done.9, bf16[256,1152]{1,0:T(8,128)(2,1)} %bitcast.319), kind=kCustom, calls=%fused_computation.7 | custom fusion | bytes 1771520 | tf_op jit(solution)/shard_map/scatter | solution.py:229
  879.0 26.6 %scatter_fusion.1 = bf16[2,256,1152]{2,1,0:T(8,128)(2,1)S(1)} fusion(bf16[2,256,1152]{2,1,0:T(8,128)(2,1)S(1)} %copy-done.1, s32[256]{0:T(256)S(1)} %copy-done.9, bf16[256,1152]{1,0:T(8,128)(2,1)} %bitcast.320), kind=kCustom, calls=%fused_computation.5 | custom fusion | bytes 1771520 | tf_op jit(solution)/shard_map/scatter | solution.py:132
  906.9 63.9 %all-reduce.2 = (f32[6912]{0:T(1024)}, f32[2,576]{1,0:T(2,128)}, f32[1152]{0:T(1024)}, f32[2304]{0:T(1024)}, f32[1152]{0:T(1024)}) all-reduce(f32[6912]{0:T(1024)} %add.447, f32[2,576]{1,0:T(2,128)} %add.449, f32[1152]{0:T(1024)} %add.451, f32[2304]{0:T(1024)S(1)} %copy-done.118, f32[1152]{0:T(1024)} %add.455), channel_id=1, replica_groups=mesh['dp'=16,'mp'=2] {'dp'}, use_global_device_ids=true, to_apply=%region_50.52 | all-reduce | flops 12672 | bytes 101376 | tf_op jit(solution)/shard_map/psum | solution.py:314
  975.3 6.7 all-reduce.5.cloned.1.call-done
  984.1 67.8 %reduce-scatter.37.cloned.1.call-done = f32[576,72]{0,1:T(8,128)} async-done(((f32[576,1152]{0,1:T(8,128)}), f32[576,72]{0,1:T(8,128)}) %reduce-scatter.37.cloned.1.call-update) | async-done | bytes 165904
  1052.0 123.8 %reduce-scatter.35.cloned.1.call-done = f32[2304,72]{0,1:T(8,128)} async-done(((f32[2304,1152]{0,1:T(8,128)}), f32[2304,72]{0,1:T(8,128)}) %reduce-scatter.35.cloned.1.call-update) | async-done | bytes 663568 | tf_op jit(solution)/shard_map/reduce_scatter | solution.py:46
  1175.8 124.6 %reduce-scatter.33.cloned.1.call-done = f32[72,2304]{1,0:T(8,128)} async-done(((f32[1152,2304]{1,0:T(8,128)}), f32[72,2304]{1,0:T(8,128)}) %reduce-scatter.33.cloned.1.call-update) | async-done | bytes 663568 | tf_op jit(solution)/shard_map/reduce_scatter | solution.py:45
  1300.4 324.4 %reduce-scatter.31.cloned.1.call-done = f32[72,6912]{1,0:T(8,128)} async-done(((f32[1152,6912]{1,0:T(8,128)}), f32[72,6912]{1,0:T(8,128)}) %reduce-scatter.31.cloned.1.call-update) | async-done | bytes 1990672 | tf_op jit(solution)/shard_map/reduce_scatter | solution.py:42
  (581 shorter events, 217.8 us)
Async XLA Ops:
  7.2 127.3 %all-gather.14.cloned.1.call-start = ((), (), s32[]{:S(2)}) async-start(), calls=%async_computation.12 | async-start | bytes 16920576 | tf_op jit(solution)/shard_map/all_gather | solution.py:32
  8.0 178.7 %all-gather.16.cloned.1.call-start = ((), (), s32[]{:S(2)}) async-start(), calls=%async_computation.13 | async-start | bytes 4700160 | tf_op jit(solution)/shard_map/all_gather | solution.py:33
  8.7 218.0 %all-gather.18.cloned.1.call-start = ((), (), s32[]{:S(2)}) async-start(), calls=%async_computation.14 | async-start | bytes 1566720 | tf_op jit(solution)/shard_map/all_gather | solution.py:34
  9.4 241.0 %reduce-scatter.15.cloned.1.call-start = ((), (), s32[]{:S(2)}) async-start(), calls=%async_computation.15 | async-start | bytes 1769472 | tf_op jit(solution)/shard_map/reduce_scatter | solution.py:26
  9.5 177.1 %copy-start.104 = (pred[2,128]{1,0:T(4,128)(4,1)}, pred[2,128]{1,0:T(4,128)(4,1)S(1)}, u32[]{:S(2)}) copy-start(pred[2,128]{1,0:T(4,128)(4,1)S(1)} %get-tuple-element.124) | copy-start | bytes 772
  9.5 254.7 %copy-start.110 = (pred[2,128]{1,0:T(4,128)(4,1)}, pred[2,128]{1,0:T(4,128)(4,1)S(1)}, u32[]{:S(2)}) copy-start(pred[2,128]{1,0:T(4,128)(4,1)S(1)} %get-tuple-element.125) | copy-start | bytes 772
  11.0 180.6 %copy-start.148 = (pred[2,128]{1,0:T(4,128)(4,1)}, pred[2,128]{1,0:T(4,128)(4,1)S(1)}, u32[]{:S(2)}) copy-start(pred[2,128]{1,0:T(4,128)(4,1)S(1)} %iota_compare_fusion.2) | copy-start | bytes 772
  11.1 181.8 %copy-start.124 = (f32[8,72]{1,0:T(8,128)}, f32[8,72]{1,0:T(8,128)S(1)}, u32[]{:S(2)}) copy-start(f32[8,72]{1,0:T(8,128)S(1)} %add.391) | copy-start | bytes 6916
  11.1 180.4 %copy-start.93 = (f32[8,72]{1,0:T(8,128)}, f32[8,72]{1,0:T(8,128)S(1)}, u32[]{:S(2)}) copy-start(f32[8,72]{1,0:T(8,128)S(1)} %add.394) | copy-start | bytes 6916
  13.0 240.2 %copy-start = (bf16[2,256,1152]{2,1,0:T(8,128)(2,1)}, bf16[2,256,1152]{2,1,0:T(8,128)(2,1)S(1)}, u32[]{:S(2)}) copy-start(bf16[2,256,1152]{2,1,0:T(8,128)(2,1)S(1)} %get-tuple-element.99) | copy-start | bytes 3538948
  229.7 45.0 %all-gather.20.cloned.1.call-start = ((), (), s32[]{:S(2)}) async-start(), calls=%async_computation.16 | async-start | bytes 1769472 | tf_op jit(solution)/shard_map/all_gather | solution.py:27
  250.5 82.9 %all-gather.22.cloned.1.call-start = ((), (), s32[]{:S(2)}) async-start(), calls=%async_computation.17 | async-start | bytes 5640192 | tf_op jit(solution)/shard_map/all_gather | solution.py:35
  251.0 139.7 %all-gather.24.cloned.1.call-start = ((), (), s32[]{:S(2)}) async-start(), calls=%async_computation.18 | async-start | bytes 5640192 | tf_op jit(solution)/shard_map/all_gather | solution.py:36
  251.8 171.6 %reduce-scatter.23.cloned.1.call-start = ((), (), s32[]{:S(2)}) async-start(), calls=%async_computation.25 | async-start | bytes 1769472 | tf_op jit(solution)/shard_map/reduce_scatter | solution.py:26
  401.6 45.1 %reduce-scatter.19.cloned.1.call-start = ((), (), s32[]{:S(2)}) async-start(), calls=%async_computation.21 | async-start | bytes 1769472 | tf_op jit(solution)/shard_map/reduce_scatter | solution.py:26
  423.3 47.6 %all-gather.32.cloned.1.call-start = ((), (), s32[]{:S(2)}) async-start(), calls=%async_computation.26 | async-start | bytes 1769472 | tf_op jit(solution)/shard_map/all_gather | solution.py:27
  423.9 71.4 %all-gather.28.cloned.1.call-start = ((), (), s32[]{:S(2)}) async-start(), calls=%async_computation.22 | async-start | bytes 1769472 | tf_op jit(solution)/shard_map/all_gather | solution.py:27
  446.7 92.5 %reduce-scatter.27.cloned.1.call-start = ((), (), s32[]{:S(2)}) async-start(), calls=%async_computation.29 | async-start | bytes 1769472 | tf_op jit(solution)/shard_map/reduce_scatter | solution.py:26
  517.2 48.6 %all-gather.36.cloned.1.call-start = ((), (), s32[]{:S(2)}) async-start(), calls=%async_computation.30 | async-start | bytes 1769472 | tf_op jit(solution)/shard_map/all_gather | solution.py:27
  539.2 48.2 %reduce-scatter.17.cloned.1.call-start = ((), (), s32[]{:S(2)}) async-start(), calls=%async_computation.19 | async-start | bytes 1769472 | tf_op jit(solution)/shard_map/reduce_scatter | solution.py:26
  545.2 66.2 %reduce-scatter.25.cloned.1.call-start = ((), (), s32[]{:S(2)}) async-start(), calls=%async_computation.27 | async-start | bytes 1769472 | tf_op jit(solution)/shard_map/reduce_scatter | solution.py:26
  558.4 77.4 %reduce-scatter.21.cloned.1.call-start = ((), (), s32[]{:S(2)}) async-start(), calls=%async_computation.23 | async-start | bytes 1769472 | tf_op jit(solution)/shard_map/reduce_scatter | solution.py:26
  565.7 94.0 %reduce-scatter.29.cloned.1.call-start = ((), (), s32[]{:S(2)}) async-start(), calls=%async_computation.31 | async-start | bytes 1769472 | tf_op jit(solution)/shard_map/reduce_scatter | solution.py:26
  584.0 123.2 %all-gather.26.cloned.1.call-start = ((), (), s32[]{:S(2)}) async-start(), calls=%async_computation.20 | async-start | bytes 1769472 | tf_op jit(solution)/shard_map/all_gather | solution.py:27
  587.4 120.9 %all-gather.34.cloned.1.call-start = ((), (), s32[]{:S(2)}) async-start(), calls=%async_computation.28 | async-start | bytes 1769472 | tf_op jit(solution)/shard_map/all_gather | solution.py:27
  611.4 121.2 %all-gather.30.cloned.1.call-start = ((), (), s32[]{:S(2)}) async-start(), calls=%async_computation.24 | async-start | bytes 1769472 | tf_op jit(solution)/shard_map/all_gather | solution.py:27
  635.8 121.1 %all-gather.38.cloned.1.call-start = ((), (), s32[]{:S(2)}) async-start(), calls=%async_computation.32 | async-start | bytes 1769472 | tf_op jit(solution)/shard_map/all_gather | solution.py:27
  659.8 322.3 %all-reduce.5.cloned.1.call-start = ((), (), s32[]{:S(2)}) async-start(), calls=%async_computation.36 | async-start | bytes 23592960
  681.7 370.3 %reduce-scatter.37.cloned.1.call-start = ((), (), s32[]{:S(2)}) async-start(), calls=%async_computation.37 | async-start | bytes 3133440
  686.7 489.1 %reduce-scatter.35.cloned.1.call-start = ((), (), s32[]{:S(2)}) async-start(), calls=%async_computation.35 | async-start | bytes 11280384 | tf_op jit(solution)/shard_map/reduce_scatter | solution.py:46
  696.1 604.3 %reduce-scatter.33.cloned.1.call-start = ((), (), s32[]{:S(2)}) async-start(), calls=%async_computation.34 | async-start | bytes 11280384 | tf_op jit(solution)/shard_map/reduce_scatter | solution.py:45
  705.4 919.4 %reduce-scatter.31.cloned.1.call-start = ((), (), s32[]{:S(2)}) async-start(), calls=%async_computation.33 | async-start | bytes 33841152 | tf_op jit(solution)/shard_map/reduce_scatter | solution.py:42
  (180 other events, 2440.9 us)
Sparse Core Ops, SparseCore 0:
  10.2 124.2 all-gather.13
  136.7 49.9 all-gather.15
  188.8 37.8 all-gather.17
  229.8 20.5 reduce-scatter.14
  251.9 22.7 all-gather.19
  277.0 56.3 all-gather.21
  335.8 54.9 all-gather.23
  401.7 20.3 reduce-scatter.22
  424.9 21.7 reduce-scatter.18
  448.1 22.7 all-gather.31
  472.6 22.7 all-gather.27
  517.4 21.7 reduce-scatter.26
  540.7 22.7 all-gather.35
  565.6 21.7 reduce-scatter.16
  589.6 21.7 reduce-scatter.24
  614.0 21.7 reduce-scatter.20
  638.0 21.7 reduce-scatter.28
  661.2 22.7 all-gather.25
  685.5 22.7 all-gather.33
  709.7 22.7 all-gather.29
  734.1 22.7 all-gather.37
  760.6 221.4 all-reduce.4
  986.6 65.3 reduce-scatter.36
  1056.5 119.2 reduce-scatter.34
  1180.4 119.9 reduce-scatter.32
  1305.1 319.6 reduce-scatter.30
where the time goes:
time: 1640 us; the launch traced here: 1630 us
  waiting for transfers between devices  1160 us (71%)
  local copies, waits for them, and re-layouts  166 us (10%)
  matrix products  159 us (10%)
  blocking collectives  63.9 us (4%)
  other arithmetic  58.5 us (4%)
  between operations  17.8 us (1%)
    reduce_scatter x1, waiting for transfers between devices, scatter_every(): lax.psum_scatter(terms[0], 'dp', scatter_dimension=0, tiled=True)  324 us
    reduce_scatter x8, waiting for transfers between devices, model_total_sum(): lax.psum_scatter(partial_value, 'mp', scatter_dimension=2, tiled=True)  133 us
    reduce_scatter x1, waiting for transfers between devices, scatter_every(): lax.psum_scatter(terms[3], 'dp', scatter_dimension=0, tiled=True)  125 us
    reduce_scatter x1, waiting for transfers between devices, scatter_every(): lax.psum_scatter(terms[4], 'dp', scatter_dimension=1, tiled=True)  124 us
    all_gather x1, waiting for transfers between devices, gather_weights(): lax.all_gather(modulation_weight, 'dp', axis=0, tiled=True)  116 us
    all_gather x8, waiting for transfers between devices, model_total_sum(): return lax.all_gather(share, 'mp', axis=2, tiled=True)  79.1 us
    unnamed x28, waiting for transfers between devices  78.7 us
    psum x1, blocking collectives, body(): lax.psum((bias_sums[0], bias_sums[1], bias_sums[2], bias_sums[3], bias_su...  63.9 us
  transfers between devices with their start and end apart: 26, of which 23 were waited for; matrix products, arithmetic and copies ran while one was open for 21% of the time, Pallas kernels for 0%

commit v1 on v0

--- a/solution.py
+++ b/solution.py
@@ -1,3 +1,4 @@
+import functools
 import jax
 import jax.numpy as jnp
 from jax import lax
@@ -8,6 +9,26 @@
 EPSILON = 1e-06
 
 
+def reach_the_rounds(local_values, which_axis):
+    reached = lax.psum(1, axis_name=which_axis)
+    w2 = lax.axis_index(which_axis)
+    new, passed = (reached, w2)
+    z_new, f_now = (local_values, 1)
+    while f_now < new:
+        block_out = range(new)
+        vec_out = map(lambda ix: (ix, ix ^ f_now), block_out)
+        t1 = list(vec_out)
+        q_next = lax.ppermute(z_new, which_axis, t1)
+        seen_now = jnp.concatenate([z_new, q_next], axis=2)
+        w1 = jnp.concatenate([q_next, z_new], axis=2)
+        z_new = jnp.where(passed & f_now == 0, seen_now, w1)
+        f_now = 2 * f_now
+    return z_new
+
+
+state_the_sites = functools.partial(reach_the_rounds, which_axis="mp")
+
+
 def normalize(rows):
     center = rows - jnp.mean(rows, axis=-1, keepdims=True)
     spread = jnp.mean(center * center, axis=-1, keepdims=True)
@@ -24,7 +45,7 @@
 
 def model_total_sum(partial_value):
     share = lax.psum_scatter(partial_value, "mp", scatter_dimension=2, tiled=True)
-    return lax.all_gather(share, "mp", axis=2, tiled=True)
+    return state_the_sites(share)
 
 
 def gather_weights(modulation_weight, input_weight, output_weight, expand_weight, shrink_weight):

time: 1640 us -> 1460 us (0.89)
  waiting for transfers between devices: 1160 us -> 961 us
    reduce_scatter x8, waiting for transfers between devices: 133 us -> 45.3 us  [model_total_sum(): lax.psum_scatter(partial_value, 'mp', scatter_dimension=2, tiled=True)]
    all_gather x8 -> x0, waiting for transfers between devices: 79.1 us -> none  [model_total_sum(): return lax.all_gather(share, 'mp', axis=2, tiled=True)]
    unnamed x28 -> x20, waiting for transfers between devices: 78.7 us -> 7.05 us
    ppermute x0 -> x8, waiting for transfers between devices: none -> 58.1 us  [reach_the_rounds(): q_next = lax.ppermute(z_new, which_axis, t1)]
    all_gather x1, waiting for transfers between devices: 54.9 us -> 37.3 us  [gather_weights(): lax.all_gather(expand_weight, 'dp', axis=0, tiled=True)]
  transfers between devices with their start and end apart: 26 -> 26, of which waited for: 23 -> 19; matrix products, arithmetic and copies ran while one was open for 21% -> 25% of each run, Pallas kernels for 0% -> 0%
where the time goes in v1:
time: 1460 us; the launch traced here: 1440 us
  waiting for transfers between devices  961 us (66%)
  local copies, waits for them, and re-layouts  173 us (12%)
  matrix products  153 us (10%)
  other arithmetic  64.8 us (4%)
  blocking collectives  62.7 us (4%)
  between operations  18.1 us (1%)
    reduce_scatter x1, waiting for transfers between devices, scatter_every(): lax.psum_scatter(terms[0], 'dp', scatter_dimension=0, tiled=True)  325 us
    reduce_scatter x1, waiting for transfers between devices, scatter_every(): lax.psum_scatter(terms[3], 'dp', scatter_dimension=0, tiled=True)  124 us
    reduce_scatter x1, waiting for transfers between devices, scatter_every(): lax.psum_scatter(terms[4], 'dp', scatter_dimension=1, tiled=True)  124 us
    all_gather x1, waiting for transfers between devices, gather_weights(): lax.all_gather(modulation_weight, 'dp', axis=0, tiled=True)  112 us
    psum x1, blocking collectives, body(): lax.psum((bias_sums[0], bias_sums[1], bias_sums[2], bias_sums[3], bias_su...  62.7 us
    ppermute x8, waiting for transfers between devices, reach_the_rounds(): q_next = lax.ppermute(z_new, which_axis, t1)  58.1 us
    scatter x2, local copies, waits for them, and re-layouts, run_micro(): block_mb = tokens_mb.at[batch_rows, order_mb].set(routed_out.astype(bf16))  53.3 us
    scatter x2, local copies, waits for them, and re-layouts, run_micro(): grad_mb.at[batch_rows, order_mb].set(grad_total.astype(bf16))  53.1 us
  transfers between devices with their start and end apart: 26, of which 19 were waited for; matrix products, arithmetic and copies ran while one was open for 25% of the time, Pallas kernels for 0%

profile of v1, /device:TPU:0, one launch (start us, length us, event | category | flops | bytes accessed | tf_op | source)
XLA Modules:
  0.0 1441.0 jit_solution(16123866024744263452)
XLA Ops:
  22.3 112.2 %all-gather.6.cloned.1.call-done = bf16[1152,6912]{1,0:T(8,128)(2,1)} async-done(((bf16[72,6912]{1,0:T(8,128)(2,1)}), bf16[1152,6912]{1,0:T(8,128)(2,1)}) %all-gather.6.cloned.1.call-update) | async-done | bytes 15925264 | tf_op jit(solution)/shard_map/all_gather | solution.py:53
  134.5 7.7 convolution_add_fusion.1
  142.9 43.7 %all-gather.8.cloned.1.call-done = bf16[3,1152,576]{2,1,0:T(8,128)(2,1)} async-done(((bf16[3,72,576]{2,1,0:T(8,128)(2,1)}), bf16[3,1152,576]{2,1,0:T(8,128)(2,1)}) %all-gather.8.cloned.1.call-update) | async-done | bytes 3981328 | tf_op jit(solution)/shard_map/all_gather | solution.py:54
  193.8 32.9 %all-gather.10.cloned.1.call-done = bf16[576,1152]{0,1:T(8,128)(2,1)} async-done(((bf16[576,72]{0,1:T(8,128)(2,1)}), bf16[576,1152]{0,1:T(8,128)(2,1)}) %all-gather.10.cloned.1.call-update) | async-done | bytes 1327120 | tf_op jit(solution)/shard_map/all_gather | solution.py:55
  229.8 8.1 convolution_add_fusion.2
  251.6 28.2 %reduce-scatter.15.cloned.1.call-done = f32[2,128,576]{1,2,0:T(8,128)} async-done(((f32[2,128,1152]{1,2,0:T(8,128)}), f32[2,128,576]{1,2,0:T(8,128)}) %reduce-scatter.15.cloned.1.call-update) | async-done | bytes 589840 | tf_op jit(solution)/shard_map/reduce_scatter | solution.py:47
  290.3 5.1 collective-permute-done
  300.6 37.3 %all-gather.12.cloned.1.call-done = bf16[1152,2304]{1,0:T(8,128)(2,1)} async-done(((bf16[72,2304]{1,0:T(8,128)(2,1)}), bf16[1152,2304]{1,0:T(8,128)(2,1)}) %all-gather.12.cloned.1.call-update) | async-done | bytes 5308432 | tf_op jit(solution)/shard_map/all_gather | solution.py:56
  338.0 5.9 fusion.27
  343.9 51.2 %all-gather.14.cloned.1.call-done = bf16[2304,1152]{0,1:T(8,128)(2,1)} async-done(((bf16[2304,72]{0,1:T(8,128)(2,1)}), bf16[2304,1152]{0,1:T(8,128)(2,1)}) %all-gather.14.cloned.1.call-update) | async-done | bytes 5308432 | tf_op jit(solution)/shard_map/all_gather | solution.py:57
  395.1 7.0 fusion.202
  427.4 5.9 fusion.9
  437.6 5.9 fusion.7
  443.8 17.0 %reduce-scatter.27.cloned.1.call-done = f32[2,128,576]{1,2,0:T(8,128)} async-done(((f32[2,128,1152]{1,2,0:T(8,128)}), f32[2,128,576]{1,2,0:T(8,128)}) %reduce-scatter.27.cloned.1.call-update) | async-done | bytes 589840 | tf_op jit(solution)/shard_map/reduce_scatter | solution.py:47
  467.9 11.6 collective-permute-done.6
  522.7 13.8 copy.156
  545.7 5.5 fusion
  554.8 5.2 fusion.1
  564.1 14.6 %collective-permute-done.1 = f32[2,128,576]{1,2,0:T(8,128)} collective-permute-done((f32[2,128,576]{1,2,0:T(8,128)}, f32[2,128,576]{1,2,0:T(8,128)}, u32[]{:S(2)}, u32[]{:S(2)}) %collective-permute-start.1) | collective-permute-done | bytes 589856 | tf_op jit(solution)/shard_map/ppermute | solution.py:21
  582.9 8.4 collective-permute-done.3
  595.4 8.6 collective-permute-done.5
  606.0 8.5 collective-permute-done.7
  620.1 12.8 fusion.182
  632.9 24.0 %convolution_add_fusion = f32[1152,6912]{1,0:T(8,128)} fusion(f32[1152,6912]{1,0:T(8,128)} %fusion.182, bf16[2,6912]{1,0:T(2,128)(2,1)S(1)} %bitcast.367, bf16[4,1152]{1,0:T(4,128)(2,1)S(1)} %copy-done.80), kind=kOutput, calls=%fused_computation.8 | convolution fusion | flops 39826944 | bytes 63733248 | tf_op jit(solution)/shard_map/bd,be->de/dot_general | solution.py:324
  661.6 26.6 %scatter_fusion = bf16[2,256,1152]{2,1,0:T(8,128)(2,1)S(1)} fusion(bf16[2,256,1152]{2,1,0:T(8,128)(2,1)S(1)} %copy-done.3, s32[256]{0:T(256)S(1)} %copy-done.11, bf16[256,1152]{1,0:T(8,128)(2,1)} %bitcast.324), kind=kCustom, calls=%fused_computation.4 | custom fusion | bytes 1771520 | tf_op jit(solution)/shard_map/scatter | solution.py:153
  688.8 26.7 %scatter_fusion.1 = bf16[2,256,1152]{2,1,0:T(8,128)(2,1)S(1)} fusion(bf16[2,256,1152]{2,1,0:T(8,128)(2,1)S(1)} %copy-done.1, s32[256]{0:T(256)S(1)} %copy-done.10, bf16[256,1152]{1,0:T(8,128)(2,1)} %bitcast.323), kind=kCustom, calls=%fused_computation.5 | custom fusion | bytes 1771520 | tf_op jit(solution)/shard_map/scatter | solution.py:153
  725.9 26.6 %scatter_fusion.2 = bf16[2,256,1152]{2,1,0:T(8,128)(2,1)S(1)} fusion(bf16[2,256,1152]{2,1,0:T(8,128)(2,1)S(1)} %copy-done.7, s32[256]{0:T(256)S(1)} %copy-done.11, bf16[256,1152]{1,0:T(8,128)(2,1)} %bitcast.325), kind=kCustom, calls=%fused_computation.6 | custom fusion | bytes 1771520 | tf_op jit(solution)/shard_map/scatter | solution.py:250
  759.4 26.6 %scatter_fusion.3 = bf16[2,256,1152]{2,1,0:T(8,128)(2,1)S(1)} fusion(bf16[2,256,1152]{2,1,0:T(8,128)(2,1)S(1)} %copy-done.5, s32[256]{0:T(256)S(1)} %copy-done.10, bf16[256,1152]{1,0:T(8,128)(2,1)} %bitcast.326), kind=kCustom, calls=%fused_computation.7 | custom fusion | bytes 1771520 | tf_op jit(solution)/shard_map/scatter | solution.py:250
  788.8 62.7 %all-reduce.2 = (f32[6912]{0:T(1024)}, f32[2,576]{1,0:T(2,128)}, f32[1152]{0:T(1024)}, f32[2304]{0:T(1024)}, f32[1152]{0:T(1024)}) all-reduce(f32[6912]{0:T(1024)} %add.447, f32[2,576]{1,0:T(2,128)} %add.449, f32[1152]{0:T(1024)} %add.451, f32[2304]{0:T(1024)S(1)} %copy-done.124, f32[1152]{0:T(1024)} %add.455), channel_id=1, replica_groups=mesh['dp'=16,'mp'=2] {'dp'}, use_global_device_ids=true, to_apply=%region_50.52 | all-reduce | flops 12672 | bytes 101376 | tf_op jit(solution)/shard_map/psum | solution.py:335
  860.6 123.8 %reduce-scatter.35.cloned.1.call-done = f32[2304,72]{0,1:T(8,128)} async-done(((f32[2304,1152]{0,1:T(8,128)}), f32[2304,72]{0,1:T(8,128)}) %reduce-scatter.35.cloned.1.call-update) | async-done | bytes 663568 | tf_op jit(solution)/shard_map/reduce_scatter | solution.py:67
  984.4 124.5 %reduce-scatter.33.cloned.1.call-done = f32[72,2304]{1,0:T(8,128)} async-done(((f32[1152,2304]{1,0:T(8,128)}), f32[72,2304]{1,0:T(8,128)}) %reduce-scatter.33.cloned.1.call-update) | async-done | bytes 663568 | tf_op jit(solution)/shard_map/reduce_scatter | solution.py:66
  1108.9 325.1 %reduce-scatter.31.cloned.1.call-done = f32[72,6912]{1,0:T(8,128)} async-done(((f32[1152,6912]{1,0:T(8,128)}), f32[72,6912]{1,0:T(8,128)}) %reduce-scatter.31.cloned.1.call-update) | async-done | bytes 1990672 | tf_op jit(solution)/shard_map/reduce_scatter | solution.py:63
  (587 shorter events, 199.3 us)
Async XLA Ops:
  7.2 127.3 %all-gather.6.cloned.1.call-start = ((), (), s32[]{:S(2)}) async-start(), calls=%async_computation.12 | async-start | bytes 16920576 | tf_op jit(solution)/shard_map/all_gather | solution.py:53
  8.0 178.7 %all-gather.8.cloned.1.call-start = ((), (), s32[]{:S(2)}) async-start(), calls=%async_computation.13 | async-start | bytes 4700160 | tf_op jit(solution)/shard_map/all_gather | solution.py:54
  8.7 218.0 %all-gather.10.cloned.1.call-start = ((), (), s32[]{:S(2)}) async-start(), calls=%async_computation.14 | async-start | bytes 1566720 | tf_op jit(solution)/shard_map/all_gather | solution.py:55
  9.4 241.0 %reduce-scatter.19.cloned.1.call-start = ((), (), s32[]{:S(2)}) async-start(), calls=%async_computation.19 | async-start | bytes 1769472 | tf_op jit(solution)/shard_map/reduce_scatter | solution.py:47
  9.5 228.5 %copy-start.103 = (pred[2,128]{1,0:T(4,128)(4,1)}, pred[2,128]{1,0:T(4,128)(4,1)S(1)}, u32[]{:S(2)}) copy-start(pred[2,128]{1,0:T(4,128)(4,1)S(1)} %get-tuple-element.124) | copy-start | bytes 772
  10.9 232.1 %copy-start.155 = (pred[2,128]{1,0:T(4,128)(4,1)}, pred[2,128]{1,0:T(4,128)(4,1)S(1)}, u32[]{:S(2)}) copy-start(pred[2,128]{1,0:T(4,128)(4,1)S(1)} %iota_compare_fusion.2) | copy-start | bytes 772
  11.6 232.7 %copy-start.133 = (f32[8,72]{1,0:T(8,128)}, f32[8,72]{1,0:T(8,128)S(1)}, u32[]{:S(2)}) copy-start(f32[8,72]{1,0:T(8,128)S(1)} %add.391) | copy-start | bytes 6916
  11.7 231.3 %copy-start.99 = (f32[8,72]{1,0:T(8,128)}, f32[8,72]{1,0:T(8,128)S(1)}, u32[]{:S(2)}) copy-start(f32[8,72]{1,0:T(8,128)S(1)} %add.394) | copy-start | bytes 6916
  16.9 221.1 %copy-start.14 = (bf16[2,128,1152]{1,2,0:T(8,128)(2,1)}, bf16[2,128,1152]{1,2,0:T(8,128)(2,1)S(1)}, u32[]{:S(2)}) copy-start(bf16[2,128,1152]{1,2,0:T(8,128)(2,1)S(1)} %copy.124) | copy-start | bytes 1769476
  17.1 220.9 %copy-start.130 = (f32[2,128]{1,0:T(2,128)}, f32[2,128]{1,0:T(2,128)S(1)}, u32[]{:S(2)}) copy-start(f32[2,128]{1,0:T(2,128)S(1)} %broadcast_multiply_fusion.3) | copy-start | bytes 3076
  229.7 50.1 %reduce-scatter.15.cloned.1.call-start = ((), (), s32[]{:S(2)}) async-start(), calls=%async_computation.15 | async-start | bytes 1769472 | tf_op jit(solution)/shard_map/reduce_scatter | solution.py:47
  247.5 90.4 %all-gather.12.cloned.1.call-start = ((), (), s32[]{:S(2)}) async-start(), calls=%async_computation.16 | async-start | bytes 5640192 | tf_op jit(solution)/shard_map/all_gather | solution.py:56
  248.1 147.0 %all-gather.14.cloned.1.call-start = ((), (), s32[]{:S(2)}) async-start(), calls=%async_computation.17 | async-start | bytes 5640192 | tf_op jit(solution)/shard_map/all_gather | solution.py:57
  248.9 187.2 %reduce-scatter.23.cloned.1.call-start = ((), (), s32[]{:S(2)}) async-start(), calls=%async_computation.21 | async-start | bytes 1769472 | tf_op jit(solution)/shard_map/reduce_scatter | solution.py:47
  250.4 39.8 %collective-permute-start.2 = (f32[2,128,576]{1,2,0:T(8,128)}, f32[2,128,576]{1,2,0:T(8,128)S(1)}, u32[]{:S(2)}, u32[]{:S(2)}) collective-permute-start(f32[2,128,576]{1,2,0:T(8,128)} %reduce-scatter.19.cloned.1.call-done), channel_id=1, source_target_pairs={{0,1},{1,0},{2,3},{3,2},{4,5},{5,4},{6,7},{7,6},{8,9},{9,8},{10,11... | collective-permute-start | bytes 1769480 | tf_op jit(solution)/shard_map/ppermute | solution.py:21
  279.8 15.6 %collective-permute-start = (f32[2,128,576]{1,2,0:T(8,128)}, f32[2,128,576]{1,2,0:T(8,128)}, u32[]{:S(2)}, u32[]{:S(2)}) collective-permute-start(f32[2,128,576]{1,2,0:T(8,128)} %reduce-scatter.15.cloned.1.call-done), channel_id=1, source_target_pairs={{0,1},{1,0},{2,3},{3,2},{4,5},{5,4},{6,7},{7,6},{8,9},{9,8},{10,11... | collective-permute-start | bytes 1769480 | tf_op jit(solution)/shard_map/ppermute | solution.py:21
  405.9 54.9 %reduce-scatter.27.cloned.1.call-start = ((), (), s32[]{:S(2)}) async-start(), calls=%async_computation.23 | async-start | bytes 1769472 | tf_op jit(solution)/shard_map/reduce_scatter | solution.py:47
  427.3 133.2 %reduce-scatter.17.cloned.1.call-start = ((), (), s32[]{:S(2)}) async-start(), calls=%async_computation.18 | async-start | bytes 1769472 | tf_op jit(solution)/shard_map/reduce_scatter | solution.py:47
  433.3 127.3 %reduce-scatter.21.cloned.1.call-start = ((), (), s32[]{:S(2)}) async-start(), calls=%async_computation.20 | async-start | bytes 1769472 | tf_op jit(solution)/shard_map/reduce_scatter | solution.py:47
  436.0 26.1 %collective-permute-start.4 = (f32[2,128,576]{1,2,0:T(8,128)}, f32[2,128,576]{1,2,0:T(8,128)}, u32[]{:S(2)}, u32[]{:S(2)}) collective-permute-start(f32[2,128,576]{1,2,0:T(8,128)} %reduce-scatter.23.cloned.1.call-done), channel_id=1, source_target_pairs={{0,1},{1,0},{2,3},{3,2},{4,5},{5,4},{6,7},{7,6},{8,9},{9,8},{10,11... | collective-permute-start | bytes 1769480 | tf_op jit(solution)/shard_map/ppermute | solution.py:21
  443.5 120.4 %reduce-scatter.25.cloned.1.call-start = ((), (), s32[]{:S(2)}) async-start(), calls=%async_computation.22 | async-start | bytes 1769472 | tf_op jit(solution)/shard_map/reduce_scatter | solution.py:47
  460.7 18.7 %collective-permute-start.6 = (f32[2,128,576]{1,2,0:T(8,128)}, f32[2,128,576]{1,2,0:T(8,128)S(1)}, u32[]{:S(2)}, u32[]{:S(2)}) collective-permute-start(f32[2,128,576]{1,2,0:T(8,128)} %reduce-scatter.27.cloned.1.call-done), channel_id=1, source_target_pairs={{0,1},{1,0},{2,3},{3,2},{4,5},{5,4},{6,7},{7,6},{8,9},{9,8},{10,11... | collective-permute-start | bytes 1769480 | tf_op jit(solution)/shard_map/ppermute | solution.py:21
  497.1 85.7 %reduce-scatter.29.cloned.1.call-start = ((), (), s32[]{:S(2)}) async-start(), calls=%async_computation.24 | async-start | bytes 1769472 | tf_op jit(solution)/shard_map/reduce_scatter | solution.py:47
  513.9 341.1 %all-reduce.5.cloned.1.call-start = ((), (), s32[]{:S(2)}) async-start(), calls=%async_computation.28 | async-start | bytes 23592960
  536.5 324.1 %reduce-scatter.37.cloned.1.call-start = ((), (), s32[]{:S(2)}) async-start(), calls=%async_computation.29 | async-start | bytes 3133440
  541.5 443.0 %reduce-scatter.35.cloned.1.call-start = ((), (), s32[]{:S(2)}) async-start(), calls=%async_computation.27 | async-start | bytes 11280384 | tf_op jit(solution)/shard_map/reduce_scatter | solution.py:67
  551.2 557.7 %reduce-scatter.33.cloned.1.call-start = ((), (), s32[]{:S(2)}) async-start(), calls=%async_computation.26 | async-start | bytes 11280384 | tf_op jit(solution)/shard_map/reduce_scatter | solution.py:66
  560.0 873.9 %reduce-scatter.31.cloned.1.call-start = ((), (), s32[]{:S(2)}) async-start(), calls=%async_computation.25 | async-start | bytes 33841152 | tf_op jit(solution)/shard_map/reduce_scatter | solution.py:63
  560.6 18.1 %collective-permute-start.1 = (f32[2,128,576]{1,2,0:T(8,128)}, f32[2,128,576]{1,2,0:T(8,128)}, u32[]{:S(2)}, u32[]{:S(2)}) collective-permute-start(f32[2,128,576]{1,2,0:T(8,128)} %reduce-scatter.17.cloned.1.call-done), channel_id=1, source_target_pairs={{0,1},{1,0},{2,3},{3,2},{4,5},{5,4},{6,7},{7,6},{8,9},{9,8},{10,11... | collective-permute-start | bytes 1769480 | tf_op jit(solution)/shard_map/ppermute | solution.py:21
  560.7 30.6 %collective-permute-start.3 = (f32[2,128,576]{1,2,0:T(8,128)}, f32[2,128,576]{1,2,0:T(8,128)}, u32[]{:S(2)}, u32[]{:S(2)}) collective-permute-start(f32[2,128,576]{1,2,0:T(8,128)} %reduce-scatter.21.cloned.1.call-done), channel_id=1, source_target_pairs={{0,1},{1,0},{2,3},{3,2},{4,5},{5,4},{6,7},{7,6},{8,9},{9,8},{10,11... | collective-permute-start | bytes 1769480 | tf_op jit(solution)/shard_map/ppermute | solution.py:21
  564.0 40.0 %collective-permute-start.5 = (f32[2,128,576]{1,2,0:T(8,128)}, f32[2,128,576]{1,2,0:T(8,128)}, u32[]{:S(2)}, u32[]{:S(2)}) collective-permute-start(f32[2,128,576]{1,2,0:T(8,128)} %reduce-scatter.25.cloned.1.call-done), channel_id=1, source_target_pairs={{0,1},{1,0},{2,3},{3,2},{4,5},{5,4},{6,7},{7,6},{8,9},{9,8},{10,11... | collective-permute-start | bytes 1769480 | tf_op jit(solution)/shard_map/ppermute | solution.py:21
  582.8 31.7 %collective-permute-start.7 = (f32[2,128,576]{1,2,0:T(8,128)}, f32[2,128,576]{1,2,0:T(8,128)S(1)}, u32[]{:S(2)}, u32[]{:S(2)}) collective-permute-start(f32[2,128,576]{1,2,0:T(8,128)} %reduce-scatter.29.cloned.1.call-done), channel_id=1, source_target_pairs={{0,1},{1,0},{2,3},{3,2},{4,5},{5,4},{6,7},{7,6},{8,9},{9,8},{10,11... | collective-permute-start | bytes 1769480 | tf_op jit(solution)/shard_map/ppermute | solution.py:21
  (186 other events, 2532.0 us)
Sparse Core Ops, SparseCore 0:
  10.2 124.2 all-gather.5
  136.7 49.9 all-gather.7
  188.8 37.8 all-gather.9
  229.8 20.5 reduce-scatter.18
  253.2 26.5 reduce-scatter.14
  281.9 56.0 all-gather.11
  340.1 54.9 all-gather.13
  406.0 20.3 reduce-scatter.22
  428.7 31.9 reduce-scatter.26
  462.8 26.5 reduce-scatter.16
  492.3 24.7 reduce-scatter.20
  519.2 21.7 reduce-scatter.24
  543.3 25.4 reduce-scatter.28
  572.4 218.3 all-reduce.4
  795.1 65.4 reduce-scatter.36
  865.1 119.2 reduce-scatter.34
  988.9 119.9 reduce-scatter.32
  1113.6 320.3 reduce-scatter.30
